TPU v7x, 32 devices: a whole 2x2x4 slice. The times are simulated.
32 devices in a mesh: gx: 4 (over z), gy: 8 (over y, x, core).
Axes of the slice: x: 2, y: 2, z: 4, core: 2. Of those that a mesh axis runs over, the one named last changes fastest.
Arguments:
- right_side: float32 [2048, 4096], P('gx', 'gy'), may hold values from -8 to 8
- drift_x: float32 [2048, 4096], P('gx', 'gy'), may hold values from -0.9 to 0.9
- drift_y: float32 [2048, 4096], P('gx', 'gy'), may hold values from -0.9 to 0.9
- sketch_rows: float32 [256, 2048], P(None, 'gx'), may hold values from -0.375 to 0.375
- sketch_cols: float32 [256, 4096], P(None, 'gy'), may hold values from -6 to 6
Outputs:
- solution: float32 [2048, 4096], P('gx', 'gy')
- residual: float32 [2048, 4096], P('gx', 'gy')
All inputs are finite; a program needn't handle non-finite values.
Results may differ from a plain program's by a relative error of at most 0.0003.
Values sent between devices are 32-bit elements; how exact they have to be, the bound alone decides.
A program may use at most 64 MiB of HBM per device.

v0:
```python
import jax
import jax.numpy as jnp
from jax import lax
from jax.sharding import PartitionSpec as P

ITERS = 4
shift_value = 0.05


def padded_2(cells, sides, width):
    for axis, dim in sides:
        count = lax.axis_size(axis)
        ends = count - 1
        head = lax.slice_in_dim(cells, 0, width, axis=dim)
        tail = lax.slice_in_dim(cells, cells.shape[dim] - width, cells.shape[dim], axis=dim)
        cells = jnp.concatenate(
            [
                lax.ppermute(tail, axis, [(i, (i + 1) % count) for i in range(ends)]),
                cells,
                lax.ppermute(head, axis, [((i + 1) % count, i) for i in range(ends)]),
            ],
            axis=dim,
        )
    return cells


def stencil(padded, field, drift_x, drift_y):
    upper_cells = padded[:-2, 1:-1]
    lower_cells = padded[2:, 1:-1]
    left_cells = padded[1:-1, :-2]
    right_cells = padded[1:-1, 2:]
    return (
        (4.0 + shift_value) * field
        - (1.0 + drift_x) * upper_cells
        - (1.0 - drift_x) * lower_cells
        - (1.0 + drift_y) * left_cells
        - (1.0 - drift_y) * right_cells
    )


def solve_small(hessenberg, beta_norm):
    gram_matrix = jnp.dot(hessenberg.T, hessenberg, precision=lax.Precision.HIGHEST)
    target = beta_norm * hessenberg[0]
    factor = jnp.linalg.cholesky(gram_matrix)
    count = hessenberg.shape[1]
    forward = []
    for row in range(count):
        acc = target[row]
        for col in range(row):
            acc = acc - factor[row, col] * forward[col]
        forward.append(acc / factor[row, row])
    backward = [None] * count
    for row in reversed(range(count)):
        acc = forward[row]
        for col in range(row + 1, count):
            acc = acc - factor[col, row] * backward[col]
        backward[row] = acc / factor[row, row]
    return backward


def body(right_side, drift_x, drift_y, sketch_rows, sketch_cols):

    def sketch(field):
        product = jnp.dot(field, sketch_cols.T, precision=lax.Precision.HIGHEST)
        partial_value = jnp.einsum(
            "ki,ik->k", sketch_rows, product, precision=lax.Precision.HIGHEST
        )
        return lax.psum(partial_value, ("gx", "gy"))

    first_sketch = sketch(right_side)
    beta_norm = jnp.sqrt(jnp.sum(first_sketch * first_sketch))
    basis_vectors = [right_side / beta_norm]
    sketched = [first_sketch / beta_norm]
    images = []
    columns = []
    for column in range(ITERS):
        current = basis_vectors[column]
        padded = padded_2(current, (("gx", 0), ("gy", 1)), 1)
        applied = stencil(padded, current, drift_x, drift_y)
        images.append(applied)
        sketch_image = sketch(applied)
        sketch_matrix = jnp.stack(sketched, axis=1)
        projection = jnp.dot(sketch_matrix.T, sketch_image, precision=lax.Precision.HIGHEST)
        remainder = applied
        for index_prev in range(column + 1):
            remainder = remainder - projection[index_prev] * basis_vectors[index_prev]
        remainder_sketch = sketch_image - jnp.dot(
            sketch_matrix, projection, precision=lax.Precision.HIGHEST
        )
        new_norm = jnp.sqrt(jnp.sum(remainder_sketch * remainder_sketch))
        basis_vectors.append(remainder / new_norm)
        sketched.append(remainder_sketch / new_norm)
        entries = jnp.concatenate(
            [projection, new_norm[None], jnp.zeros((ITERS - column - 1,), jnp.float32)]
        )
        columns.append(entries)
    hessenberg = jnp.stack(columns, axis=1)
    coeffs = solve_small(hessenberg, beta_norm)
    solution = jnp.zeros_like(right_side)
    for column in range(ITERS):
        solution = solution + coeffs[column] * basis_vectors[column]
    padded = padded_2(solution, (("gx", 0), ("gy", 1)), 1)
    residual = right_side - stencil(padded, solution, drift_x, drift_y)
    return (solution, residual)


def solution(mesh):
    in_specs = (P("gx", "gy"), P("gx", "gy"), P("gx", "gy"), P(None, "gx"), P(None, "gy"))
    out_specs = (P("gx", "gy"), P("gx", "gy"))
    return jax.shard_map(body, mesh=mesh, in_specs=in_specs, out_specs=out_specs, check_vma=False)
```

profile of v0, /device:TPU:1, one launch (start us, length us, event | category | flops | bytes accessed | tf_op | source)
XLA Modules:
  0.0 370.7 jit_solution(15757160799951034432)
XLA Ops:
  4.3 40.5 %psum.35 = f32[256]{0:T(256)S(1)} all-reduce(f32[256]{0:T(256)S(1)} %multiply_reduce_fusion.4), channel_id=1, replica_groups=mesh['gx'=4,'gy'=8] {'gx','gy'}, use_global_device_ids=true, to_apply=%region_0.0 | all-reduce | flops 256 | bytes 2048 | tf_op jit(solution)/shard_map/psum | solution.py:68
  46.3 3.3 collective-permute-start
  50.9 3.0 collective-permute-done.1
  54.1 6.7 %collective-permute-start.2 = (f32[514,1]{1,0:T(8,128)S(1)}, f32[514,1]{1,0:T(8,128)S(1)}, u32[]{:S(2)}, u32[]{:S(2)}) collective-permute-start(f32[514,1]{1,0:T(8,128)S(1)} %get-tuple-element.16), channel_id=1, source_target_pairs={{0,1},{1,2},{2,3},{3,4},{4,5},{5,6},{6,7},{8,9},{9,10},{10,11},{11... | collective-permute-start | bytes 6176 | tf_op jit(solution)/shard_map/ppermute | solution.py:18
  64.1 4.5 %collective-permute-done.3 = f32[514,1]{1,0:T(8,128)S(1)} collective-permute-done((f32[514,1]{1,0:T(8,128)S(1)}, f32[514,1]{1,0:T(8,128)S(1)}, u32[]{:S(2)}, u32[]{:S(2)}) %collective-permute-start.3) | collective-permute-done | bytes 2088 | tf_op jit(solution)/shard_map/ppermute | solution.py:20
  71.8 38.4 %psum.36 = f32[256]{0:T(256)S(1)} all-reduce(f32[256]{0:T(256)S(1)} %multiply_reduce_fusion.3), channel_id=1, replica_groups=mesh['gx'=4,'gy'=8] {'gx','gy'}, use_global_device_ids=true, to_apply=%region_2.0 | all-reduce | flops 256 | bytes 2048 | tf_op jit(solution)/shard_map/psum | solution.py:68
  121.8 6.7 %collective-permute-start.6 = (f32[514,1]{1,0:T(8,128)S(1)}, f32[514,1]{1,0:T(8,128)S(1)}, u32[]{:S(2)}, u32[]{:S(2)}) collective-permute-start(f32[514,1]{1,0:T(8,128)S(1)} %get-tuple-element.14), channel_id=1, source_target_pairs={{0,1},{1,2},{2,3},{3,4},{4,5},{5,6},{6,7},{8,9},{9,10},{10,11},{11... | collective-permute-start | bytes 6176 | tf_op jit(solution)/shard_map/ppermute | solution.py:18
  131.9 4.5 %collective-permute-done.7 = f32[514,1]{1,0:T(8,128)S(1)} collective-permute-done((f32[514,1]{1,0:T(8,128)S(1)}, f32[514,1]{1,0:T(8,128)S(1)}, u32[]{:S(2)}, u32[]{:S(2)}) %collective-permute-start.7) | collective-permute-done | bytes 2088 | tf_op jit(solution)/shard_map/ppermute | solution.py:20
  143.2 37.7 %psum.37 = f32[256]{0:T(256)S(1)} all-reduce(f32[256]{0:T(256)S(1)} %multiply_reduce_fusion.2), channel_id=1, replica_groups=mesh['gx'=4,'gy'=8] {'gx','gy'}, use_global_device_ids=true, to_apply=%region_4.0 | all-reduce | flops 256 | bytes 2048 | tf_op jit(solution)/shard_map/psum | solution.py:68
  183.1 2.9 subtract_divide_fusion.1
  186.0 3.1 collective-permute-start.8
  190.5 3.0 collective-permute-done.9
  193.6 6.7 %collective-permute-start.10 = (f32[514,1]{1,0:T(8,128)S(1)}, f32[514,1]{1,0:T(8,128)S(1)}, u32[]{:S(2)}, u32[]{:S(2)}) collective-permute-start(f32[514,1]{1,0:T(8,128)S(1)} %get-tuple-element.12), channel_id=1, source_target_pairs={{0,1},{1,2},{2,3},{3,4},{4,5},{5,6},{6,7},{8,9},{9,10},{10,11},{11... | collective-permute-start | bytes 6176 | tf_op jit(solution)/shard_map/ppermute | solution.py:18
  203.7 4.5 %collective-permute-done.11 = f32[514,1]{1,0:T(8,128)S(1)} collective-permute-done((f32[514,1]{1,0:T(8,128)S(1)}, f32[514,1]{1,0:T(8,128)S(1)}, u32[]{:S(2)}, u32[]{:S(2)}) %collective-permute-start.11) | collective-permute-done | bytes 2088 | tf_op jit(solution)/shard_map/ppermute | solution.py:20
  215.0 37.8 %psum.38 = f32[256]{0:T(256)S(1)} all-reduce(f32[256]{0:T(256)S(1)} %multiply_reduce_fusion.1), channel_id=1, replica_groups=mesh['gx'=4,'gy'=8] {'gx','gy'}, use_global_device_ids=true, to_apply=%region_6.0 | all-reduce | flops 256 | bytes 2048 | tf_op jit(solution)/shard_map/psum | solution.py:68
  254.9 3.9 %subtract_divide_fusion = f32[512,512]{1,0:T(8,128)S(1)} fusion(f32[512,512]{1,0:T(8,128)} %copy-done.2, f32[512,512]{1,0:T(8,128)S(1)} %subtract_divide_fusion.2, f32[512,512]{1,0:T(8,128)} %copy-done.16, f32[]{:T(128)} %sqrt.18, f32[]{:T(128)} %bitcast.31, f32[]{:T(128)} %bitcast.30, f32[]{:T(128)} %bitcast.29, f32[512,512]{1,0:T(8,128)S(1)} %copy-done.1, ...), kind=kLoop, calls=%fused_computation.92 | loop fusion | flops 2097152 | bytes 5242900 | tf_op jit(solution)/shard_map/div | solution.py:91
  258.9 3.0 collective-permute-start.12
  263.2 3.0 collective-permute-done.13
  266.4 6.7 %collective-permute-start.14 = (f32[514,1]{1,0:T(8,128)S(1)}, f32[514,1]{1,0:T(8,128)S(1)}, u32[]{:S(2)}, u32[]{:S(2)}) collective-permute-start(f32[514,1]{1,0:T(8,128)S(1)} %get-tuple-element.10), channel_id=1, source_target_pairs={{0,1},{1,2},{2,3},{3,4},{4,5},{5,6},{6,7},{8,9},{9,10},{10,11},{11... | collective-permute-start | bytes 6176 | tf_op jit(solution)/shard_map/ppermute | solution.py:18
  276.4 4.5 %collective-permute-done.15 = f32[514,1]{1,0:T(8,128)S(1)} collective-permute-done((f32[514,1]{1,0:T(8,128)S(1)}, f32[514,1]{1,0:T(8,128)S(1)}, u32[]{:S(2)}, u32[]{:S(2)}) %collective-permute-start.15) | collective-permute-done | bytes 2088 | tf_op jit(solution)/shard_map/ppermute | solution.py:20
  286.6 37.8 %psum.39 = f32[256]{0:T(256)S(1)} all-reduce(f32[256]{0:T(256)S(1)} %multiply_reduce_fusion), channel_id=1, replica_groups=mesh['gx'=4,'gy'=8] {'gx','gy'}, use_global_device_ids=true, to_apply=%region_8.0 | all-reduce | flops 256 | bytes 2048 | tf_op jit(solution)/shard_map/psum | solution.py:68
  351.1 3.0 collective-permute-done.17
  354.3 6.7 %collective-permute-start.18 = (f32[514,1]{1,0:T(8,128)S(1)}, f32[514,1]{1,0:T(8,128)S(1)}, u32[]{:S(2)}, u32[]{:S(2)}) collective-permute-start(f32[514,1]{1,0:T(8,128)S(1)} %get-tuple-element.8), channel_id=1, source_target_pairs={{0,1},{1,2},{2,3},{3,4},{4,5},{5,6},{6,7},{8,9},{9,10},{10,11},{11... | collective-permute-start | bytes 6176 | tf_op jit(solution)/shard_map/ppermute | solution.py:18
  364.3 4.5 %collective-permute-done.19 = f32[514,1]{1,0:T(8,128)S(1)} collective-permute-done((f32[514,1]{1,0:T(8,128)S(1)}, f32[514,1]{1,0:T(8,128)S(1)}, u32[]{:S(2)}, u32[]{:S(2)}) %collective-permute-start.19) | collective-permute-done | bytes 2088 | tf_op jit(solution)/shard_map/ppermute | solution.py:20
  (127 shorter events, 74.7 us)
Async XLA Ops:
  4.0 42.2 %copy-start.1 = (f32[512,512]{1,0:T(8,128)S(1)}, f32[512,512]{1,0:T(8,128)}, u32[]{:S(2)}) copy-start(f32[512,512]{1,0:T(8,128)} %param.5) | copy-start | bytes 3145732
  46.3 4.6 %collective-permute-start = (f32[1,512]{1,0:T(1,128)S(1)}, f32[1,512]{1,0:T(1,128)S(1)}, u32[]{:S(2)}, u32[]{:S(2)}) collective-permute-start(f32[1,512]{1,0:T(1,128)S(1)} %get-tuple-element.26), channel_id=1, source_target_pairs={{0,8},{8,16},{16,24},{1,9},{9,17},{17,25},{2,10},{10,18},{18,26},{... | collective-permute-start | bytes 6152 | tf_op jit(solution)/shard_map/ppermute | solution.py:18
  49.6 4.3 %collective-permute-start.1 = (f32[1,512]{1,0:T(1,128)S(1)}, f32[1,512]{1,0:T(1,128)S(1)}, u32[]{:S(2)}, u32[]{:S(2)}) collective-permute-start(f32[1,512]{1,0:T(1,128)S(1)} %get-tuple-element.27), channel_id=1, source_target_pairs={{8,0},{16,8},{24,16},{9,1},{17,9},{25,17},{10,2},{18,10},{26,18},{... | collective-permute-start | bytes 6152 | tf_op jit(solution)/shard_map/ppermute | solution.py:20
  54.1 10.1 %collective-permute-start.2 = (f32[514,1]{1,0:T(8,128)S(1)}, f32[514,1]{1,0:T(8,128)S(1)}, u32[]{:S(2)}, u32[]{:S(2)}) collective-permute-start(f32[514,1]{1,0:T(8,128)S(1)} %get-tuple-element.16), channel_id=1, source_target_pairs={{0,1},{1,2},{2,3},{3,4},{4,5},{5,6},{6,7},{8,9},{9,10},{10,11},{11... | collective-permute-start | bytes 6176 | tf_op jit(solution)/shard_map/ppermute | solution.py:18
  60.8 7.8 %collective-permute-start.3 = (f32[514,1]{1,0:T(8,128)S(1)}, f32[514,1]{1,0:T(8,128)S(1)}, u32[]{:S(2)}, u32[]{:S(2)}) collective-permute-start(f32[514,1]{1,0:T(8,128)S(1)} %get-tuple-element.17), channel_id=1, source_target_pairs={{1,0},{2,1},{3,2},{4,3},{5,4},{6,5},{7,6},{9,8},{10,9},{11,10},{12... | collective-permute-start | bytes 6176 | tf_op jit(solution)/shard_map/ppermute | solution.py:20
  115.0 4.4 %collective-permute-start.4 = (f32[1,512]{1,0:T(1,128)S(1)}, f32[1,512]{1,0:T(1,128)S(1)}, u32[]{:S(2)}, u32[]{:S(2)}) collective-permute-start(f32[1,512]{1,0:T(1,128)S(1)} %get-tuple-element.24), channel_id=1, source_target_pairs={{0,8},{8,16},{16,24},{1,9},{9,17},{17,25},{2,10},{10,18},{18,26},{... | collective-permute-start | bytes 6152 | tf_op jit(solution)/shard_map/ppermute | solution.py:18
  117.4 4.3 %collective-permute-start.5 = (f32[1,512]{1,0:T(1,128)S(1)}, f32[1,512]{1,0:T(1,128)S(1)}, u32[]{:S(2)}, u32[]{:S(2)}) collective-permute-start(f32[1,512]{1,0:T(1,128)S(1)} %get-tuple-element.25), channel_id=1, source_target_pairs={{8,0},{16,8},{24,16},{9,1},{17,9},{25,17},{10,2},{18,10},{26,18},{... | collective-permute-start | bytes 6152 | tf_op jit(solution)/shard_map/ppermute | solution.py:20
  121.8 10.1 %collective-permute-start.6 = (f32[514,1]{1,0:T(8,128)S(1)}, f32[514,1]{1,0:T(8,128)S(1)}, u32[]{:S(2)}, u32[]{:S(2)}) collective-permute-start(f32[514,1]{1,0:T(8,128)S(1)} %get-tuple-element.14), channel_id=1, source_target_pairs={{0,1},{1,2},{2,3},{3,4},{4,5},{5,6},{6,7},{8,9},{9,10},{10,11},{11... | collective-permute-start | bytes 6176 | tf_op jit(solution)/shard_map/ppermute | solution.py:18
  128.6 7.8 %collective-permute-start.7 = (f32[514,1]{1,0:T(8,128)S(1)}, f32[514,1]{1,0:T(8,128)S(1)}, u32[]{:S(2)}, u32[]{:S(2)}) collective-permute-start(f32[514,1]{1,0:T(8,128)S(1)} %get-tuple-element.15), channel_id=1, source_target_pairs={{1,0},{2,1},{3,2},{4,3},{5,4},{6,5},{7,6},{9,8},{10,9},{11,10},{12... | collective-permute-start | bytes 6176 | tf_op jit(solution)/shard_map/ppermute | solution.py:20
  183.1 25.1 %copy-start.10 = (f32[512,512]{1,0:T(8,128)S(1)}, f32[512,512]{1,0:T(8,128)}, u32[]{:S(2)}) copy-start(f32[512,512]{1,0:T(8,128)} %param.6) | copy-start | bytes 3145732
  186.0 4.4 %collective-permute-start.8 = (f32[1,512]{1,0:T(1,128)S(1)}, f32[1,512]{1,0:T(1,128)S(1)}, u32[]{:S(2)}, u32[]{:S(2)}) collective-permute-start(f32[1,512]{1,0:T(1,128)S(1)} %get-tuple-element.22), channel_id=1, source_target_pairs={{0,8},{8,16},{16,24},{1,9},{9,17},{17,25},{2,10},{10,18},{18,26},{... | collective-permute-start | bytes 6152 | tf_op jit(solution)/shard_map/ppermute | solution.py:18
  189.1 4.3 %collective-permute-start.9 = (f32[1,512]{1,0:T(1,128)S(1)}, f32[1,512]{1,0:T(1,128)S(1)}, u32[]{:S(2)}, u32[]{:S(2)}) collective-permute-start(f32[1,512]{1,0:T(1,128)S(1)} %get-tuple-element.23), channel_id=1, source_target_pairs={{8,0},{16,8},{24,16},{9,1},{17,9},{25,17},{10,2},{18,10},{26,18},{... | collective-permute-start | bytes 6152 | tf_op jit(solution)/shard_map/ppermute | solution.py:20
  193.6 10.1 %collective-permute-start.10 = (f32[514,1]{1,0:T(8,128)S(1)}, f32[514,1]{1,0:T(8,128)S(1)}, u32[]{:S(2)}, u32[]{:S(2)}) collective-permute-start(f32[514,1]{1,0:T(8,128)S(1)} %get-tuple-element.12), channel_id=1, source_target_pairs={{0,1},{1,2},{2,3},{3,4},{4,5},{5,6},{6,7},{8,9},{9,10},{10,11},{11... | collective-permute-start | bytes 6176 | tf_op jit(solution)/shard_map/ppermute | solution.py:18
  200.3 7.8 %collective-permute-start.11 = (f32[514,1]{1,0:T(8,128)S(1)}, f32[514,1]{1,0:T(8,128)S(1)}, u32[]{:S(2)}, u32[]{:S(2)}) collective-permute-start(f32[514,1]{1,0:T(8,128)S(1)} %get-tuple-element.13), channel_id=1, source_target_pairs={{1,0},{2,1},{3,2},{4,3},{5,4},{6,5},{7,6},{9,8},{10,9},{11,10},{12... | collective-permute-start | bytes 6176 | tf_op jit(solution)/shard_map/ppermute | solution.py:20
  254.9 26.0 %copy-start.11 = (f32[512,512]{1,0:T(8,128)S(1)}, f32[512,512]{1,0:T(8,128)}, u32[]{:S(2)}) copy-start(f32[512,512]{1,0:T(8,128)} %param.6) | copy-start | bytes 3145732
  258.9 4.3 %collective-permute-start.12 = (f32[1,512]{1,0:T(1,128)S(1)}, f32[1,512]{1,0:T(1,128)S(1)}, u32[]{:S(2)}, u32[]{:S(2)}) collective-permute-start(f32[1,512]{1,0:T(1,128)S(1)} %get-tuple-element.20), channel_id=1, source_target_pairs={{0,8},{8,16},{16,24},{1,9},{9,17},{17,25},{2,10},{10,18},{18,26},{... | collective-permute-start | bytes 6152 | tf_op jit(solution)/shard_map/ppermute | solution.py:18
  261.9 4.3 %collective-permute-start.13 = (f32[1,512]{1,0:T(1,128)S(1)}, f32[1,512]{1,0:T(1,128)S(1)}, u32[]{:S(2)}, u32[]{:S(2)}) collective-permute-start(f32[1,512]{1,0:T(1,128)S(1)} %get-tuple-element.21), channel_id=1, source_target_pairs={{8,0},{16,8},{24,16},{9,1},{17,9},{25,17},{10,2},{18,10},{26,18},{... | collective-permute-start | bytes 6152 | tf_op jit(solution)/shard_map/ppermute | solution.py:20
  266.4 10.1 %collective-permute-start.14 = (f32[514,1]{1,0:T(8,128)S(1)}, f32[514,1]{1,0:T(8,128)S(1)}, u32[]{:S(2)}, u32[]{:S(2)}) collective-permute-start(f32[514,1]{1,0:T(8,128)S(1)} %get-tuple-element.10), channel_id=1, source_target_pairs={{0,1},{1,2},{2,3},{3,4},{4,5},{5,6},{6,7},{8,9},{9,10},{10,11},{11... | collective-permute-start | bytes 6176 | tf_op jit(solution)/shard_map/ppermute | solution.py:18
  273.1 7.8 %collective-permute-start.15 = (f32[514,1]{1,0:T(8,128)S(1)}, f32[514,1]{1,0:T(8,128)S(1)}, u32[]{:S(2)}, u32[]{:S(2)}) collective-permute-start(f32[514,1]{1,0:T(8,128)S(1)} %get-tuple-element.11), channel_id=1, source_target_pairs={{1,0},{2,1},{3,2},{4,3},{5,4},{6,5},{7,6},{9,8},{10,9},{11,10},{12... | collective-permute-start | bytes 6176 | tf_op jit(solution)/shard_map/ppermute | solution.py:20
  344.7 24.1 %copy-start.12 = (f32[512,512]{1,0:T(8,128)S(1)}, f32[512,512]{1,0:T(8,128)}, u32[]{:S(2)}) copy-start(f32[512,512]{1,0:T(8,128)} %param.6) | copy-start | bytes 3145732
  346.9 4.2 %collective-permute-start.16 = (f32[1,512]{1,0:T(1,128)S(1)}, f32[1,512]{1,0:T(1,128)S(1)}, u32[]{:S(2)}, u32[]{:S(2)}) collective-permute-start(f32[1,512]{1,0:T(1,128)S(1)} %get-tuple-element.18), channel_id=1, source_target_pairs={{0,8},{8,16},{16,24},{1,9},{9,17},{17,25},{2,10},{10,18},{18,26},{... | collective-permute-start | bytes 6152 | tf_op jit(solution)/shard_map/ppermute | solution.py:18
  349.8 4.3 %collective-permute-start.17 = (f32[1,512]{1,0:T(1,128)S(1)}, f32[1,512]{1,0:T(1,128)S(1)}, u32[]{:S(2)}, u32[]{:S(2)}) collective-permute-start(f32[1,512]{1,0:T(1,128)S(1)} %get-tuple-element.19), channel_id=1, source_target_pairs={{8,0},{16,8},{24,16},{9,1},{17,9},{25,17},{10,2},{18,10},{26,18},{... | collective-permute-start | bytes 6152 | tf_op jit(solution)/shard_map/ppermute | solution.py:20
  354.3 10.1 %collective-permute-start.18 = (f32[514,1]{1,0:T(8,128)S(1)}, f32[514,1]{1,0:T(8,128)S(1)}, u32[]{:S(2)}, u32[]{:S(2)}) collective-permute-start(f32[514,1]{1,0:T(8,128)S(1)} %get-tuple-element.8), channel_id=1, source_target_pairs={{0,1},{1,2},{2,3},{3,4},{4,5},{5,6},{6,7},{8,9},{9,10},{10,11},{11... | collective-permute-start | bytes 6176 | tf_op jit(solution)/shard_map/ppermute | solution.py:18
  361.0 7.8 %collective-permute-start.19 = (f32[514,1]{1,0:T(8,128)S(1)}, f32[514,1]{1,0:T(8,128)S(1)}, u32[]{:S(2)}, u32[]{:S(2)}) collective-permute-start(f32[514,1]{1,0:T(8,128)S(1)} %get-tuple-element.9), channel_id=1, source_target_pairs={{1,0},{2,1},{3,2},{4,3},{5,4},{6,5},{7,6},{9,8},{10,9},{11,10},{12... | collective-permute-start | bytes 6176 | tf_op jit(solution)/shard_map/ppermute | solution.py:20
  (15 other events, 231.2 us)
where the time goes:
time: 372 us; the launch traced here: 371 us
  blocking collectives  192 us (52%)
  starting transfers between devices  64.4 us (17%)
  waiting for transfers between devices  42.7 us (11%)
  other arithmetic  28.1 us (8%)
  between operations  19.8 us (5%)
  local copies, waits for them, and re-layouts  13.1 us (4%)
  matrix products  10.4 us (3%)
    psum x5, blocking collectives, sketch(): return lax.psum(partial_value, ('gx', 'gy'))  192 us
    ppermute x10, starting transfers between devices, padded_2(): lax.ppermute(tail, axis, [(i, (i + 1) % count) for i in range(ends)])  48.2 us
    ppermute x10, waiting for transfers between devices, padded_2(): lax.ppermute(head, axis, [((i + 1) % count, i) for i in range(ends)])  36.7 us
    ppermute x10, starting transfers between devices, padded_2(): lax.ppermute(head, axis, [((i + 1) % count, i) for i in range(ends)])  16.2 us
    unnamed x43, local copies, waits for them, and re-layouts  10.5 us
    dot_general x5, matrix products, sketch(): product = jnp.dot(field, sketch_cols.T, precision=lax.Precision.HIGHEST)  9.45 us
    div x3, other arithmetic, body(): basis_vectors.append(remainder / new_norm)  9.05 us
  transfers between devices with their start and end apart: 20, of which 15 were waited for; matrix products, arithmetic and copies ran while one was open for 0% of the time, Pallas kernels for 0%

commit v1 on v0

--- a/solution.py
+++ b/solution.py
@@ -5,6 +5,12 @@
 
 ITERS = 4
 shift_value = 0.05
+
+
+def gather_and_add(block, name):
+    parts = lax.all_gather(block, name, axis=0, tiled=False)
+    total = parts.sum(axis=0)
+    return total
 
 
 def padded_2(cells, sides, width):
@@ -65,7 +71,7 @@
         partial_value = jnp.einsum(
             "ki,ik->k", sketch_rows, product, precision=lax.Precision.HIGHEST
         )
-        return lax.psum(partial_value, ("gx", "gy"))
+        return gather_and_add(partial_value, ("gx", "gy"))
 
     first_sketch = sketch(right_side)
     beta_norm = jnp.sqrt(jnp.sum(first_sketch * first_sketch))

time: 372 us -> 341 us (0.917)
  starting transfers between devices: 64.4 us -> 36.2 us
    psum x5 -> x0, blocking collectives: 192 us -> none  [sketch(): return lax.psum(partial_value, ('gx', 'gy'))]
    all_gather x0 -> x5, blocking collectives: none -> 192 us  [gather_and_add(): parts = lax.all_gather(block, name, axis=0, tiled=False)]
    ppermute x10, starting transfers between devices: 48.2 us -> 16.7 us  [padded_2(): lax.ppermute(tail, axis, [(i, (i + 1) % count) for i in range(ends)])]
where the time goes in v1:
time: 341 us; the launch traced here: 339 us
  blocking collectives  192 us (56%)
  waiting for transfers between devices  39.9 us (12%)
  starting transfers between devices  36.2 us (11%)
  other arithmetic  27.8 us (8%)
  between operations  19.8 us (6%)
  local copies, waits for them, and re-layouts  13.2 us (4%)
  matrix products  10.4 us (3%)
    all_gather x5, blocking collectives, gather_and_add(): parts = lax.all_gather(block, name, axis=0, tiled=False)  192 us
    ppermute x10, waiting for transfers between devices, padded_2(): lax.ppermute(head, axis, [((i + 1) % count, i) for i in range(ends)])  37 us
    ppermute x10, starting transfers between devices, padded_2(): lax.ppermute(head, axis, [((i + 1) % count, i) for i in range(ends)])  19.5 us
    ppermute x10, starting transfers between devices, padded_2(): lax.ppermute(tail, axis, [(i, (i + 1) % count) for i in range(ends)])  16.7 us
    unnamed x43, local copies, waits for them, and re-layouts  10.5 us
    dot_general x5, matrix products, sketch(): product = jnp.dot(field, sketch_cols.T, precision=lax.Precision.HIGHEST)  9.44 us
    div x3, other arithmetic, body(): basis_vectors.append(remainder / new_norm)  9.04 us
  transfers between devices with their start and end apart: 20, of which 15 were waited for; matrix products, arithmetic and copies ran while one was open for 0% of the time, Pallas kernels for 0%

profile of v1, /device:TPU:1, one launch (start us, length us, event | category | flops | bytes accessed | tf_op | source)
XLA Modules:
  0.0 339.3 jit_solution(9830431276913863019)
XLA Ops:
  1.7 2.3 convolution_bitcast_fusion.4
  4.3 43.2 %all-gather.5 = f32[32,1,256]{2,1,0:T(1,128)S(1)} all-gather(f32[1,1,256]{2,1,0:T(1,128)S(1)} %bitcast.104), channel_id=2, replica_groups=mesh['gx'=4,'gy'=8] {'gx','gy'}, dimensions={0}, use_global_device_ids=true | all-gather | bytes 33792 | tf_op jit(solution)/shard_map/all_gather | solution.py:11
  51.8 3.0 collective-permute-done.1
  56.9 2.6 collective-permute-start.3
  60.2 4.4 %collective-permute-done.3 = f32[514,1]{1,0:T(8,128)S(1)} collective-permute-done((f32[514,1]{1,0:T(8,128)S(1)}, f32[514,1]{1,0:T(8,128)S(1)}, u32[]{:S(2)}, u32[]{:S(2)}) %collective-permute-start.3) | collective-permute-done | bytes 2088 | tf_op jit(solution)/shard_map/ppermute | solution.py:26
  67.8 37.2 %all-gather.6 = f32[32,1,256]{2,1,0:T(1,128)S(1)} all-gather(f32[1,1,256]{2,1,0:T(1,128)S(1)} %bitcast.105), channel_id=3, replica_groups=mesh['gx'=4,'gy'=8] {'gx','gy'}, dimensions={0}, use_global_device_ids=true | all-gather | bytes 33792 | tf_op jit(solution)/shard_map/all_gather | solution.py:11
  112.4 3.0 collective-permute-done.5
  117.5 2.6 collective-permute-start.7
  120.8 4.4 %collective-permute-done.7 = f32[514,1]{1,0:T(8,128)S(1)} collective-permute-done((f32[514,1]{1,0:T(8,128)S(1)}, f32[514,1]{1,0:T(8,128)S(1)}, u32[]{:S(2)}, u32[]{:S(2)}) %collective-permute-start.7) | collective-permute-done | bytes 2088 | tf_op jit(solution)/shard_map/ppermute | solution.py:26
  132.1 37.2 %all-gather.7 = f32[32,1,256]{2,1,0:T(1,128)S(1)} all-gather(f32[1,1,256]{2,1,0:T(1,128)S(1)} %bitcast.106), channel_id=4, replica_groups=mesh['gx'=4,'gy'=8] {'gx','gy'}, dimensions={0}, use_global_device_ids=true | all-gather | bytes 33792 | tf_op jit(solution)/shard_map/all_gather | solution.py:11
  171.5 2.9 subtract_divide_fusion.1
  177.2 3.0 collective-permute-done.9
  182.2 2.6 collective-permute-start.11
  185.6 4.4 %collective-permute-done.11 = f32[514,1]{1,0:T(8,128)S(1)} collective-permute-done((f32[514,1]{1,0:T(8,128)S(1)}, f32[514,1]{1,0:T(8,128)S(1)}, u32[]{:S(2)}, u32[]{:S(2)}) %collective-permute-start.11) | collective-permute-done | bytes 2088 | tf_op jit(solution)/shard_map/ppermute | solution.py:26
  196.8 37.3 %all-gather.8 = f32[32,1,256]{2,1,0:T(1,128)S(1)} all-gather(f32[1,1,256]{2,1,0:T(1,128)S(1)} %bitcast.107), channel_id=5, replica_groups=mesh['gx'=4,'gy'=8] {'gx','gy'}, dimensions={0}, use_global_device_ids=true | all-gather | bytes 33792 | tf_op jit(solution)/shard_map/all_gather | solution.py:11
  236.5 4.0 %subtract_divide_fusion = f32[512,512]{1,0:T(8,128)S(1)} fusion(f32[512,512]{1,0:T(8,128)} %copy-done.2, f32[512,512]{1,0:T(8,128)S(1)} %subtract_divide_fusion.2, f32[512,512]{1,0:T(8,128)} %copy-done.16, f32[]{:T(128)} %sqrt.18, f32[]{:T(128)} %bitcast.35, f32[]{:T(128)} %bitcast.34, f32[]{:T(128)} %bitcast.33, f32[512,512]{1,0:T(8,128)S(1)} %copy-done.1, ...), kind=kLoop, calls=%fused_computation.92 | loop fusion | flops 2097152 | bytes 5242900 | tf_op jit(solution)/shard_map/div | solution.py:97
  243.3 3.0 collective-permute-done.13
  248.3 2.6 collective-permute-start.15
  251.7 4.4 %collective-permute-done.15 = f32[514,1]{1,0:T(8,128)S(1)} collective-permute-done((f32[514,1]{1,0:T(8,128)S(1)}, f32[514,1]{1,0:T(8,128)S(1)}, u32[]{:S(2)}, u32[]{:S(2)}) %collective-permute-start.15) | collective-permute-done | bytes 2088 | tf_op jit(solution)/shard_map/ppermute | solution.py:26
  256.1 2.5 convolution_bitcast_fusion
  261.8 37.2 %all-gather.9 = f32[32,1,256]{2,1,0:T(1,128)S(1)} all-gather(f32[1,1,256]{2,1,0:T(1,128)S(1)} %bitcast.108), channel_id=6, replica_groups=mesh['gx'=4,'gy'=8] {'gx','gy'}, dimensions={0}, use_global_device_ids=true | all-gather | bytes 33792 | tf_op jit(solution)/shard_map/all_gather | solution.py:11
  324.6 3.0 collective-permute-done.17
  329.7 2.6 collective-permute-start.19
  333.0 4.4 %collective-permute-done.19 = f32[514,1]{1,0:T(8,128)S(1)} collective-permute-done((f32[514,1]{1,0:T(8,128)S(1)}, f32[514,1]{1,0:T(8,128)S(1)}, u32[]{:S(2)}, u32[]{:S(2)}) %collective-permute-start.19) | collective-permute-done | bytes 2088 | tf_op jit(solution)/shard_map/ppermute | solution.py:26
  (131 shorter events, 65.7 us)
Async XLA Ops:
  4.0 44.9 %copy-start.1 = (f32[512,512]{1,0:T(8,128)S(1)}, f32[512,512]{1,0:T(8,128)}, u32[]{:S(2)}) copy-start(f32[512,512]{1,0:T(8,128)} %param.5) | copy-start | bytes 3145732
  49.1 2.7 collective-permute-start
  50.5 4.3 %collective-permute-start.1 = (f32[1,512]{1,0:T(1,128)S(1)}, f32[1,512]{1,0:T(1,128)S(1)}, u32[]{:S(2)}, u32[]{:S(2)}) collective-permute-start(f32[1,512]{1,0:T(1,128)S(1)} %get-tuple-element.27), channel_id=1, source_target_pairs={{8,0},{16,8},{24,16},{9,1},{17,9},{25,17},{10,2},{18,10},{26,18},{... | collective-permute-start | bytes 6152 | tf_op jit(solution)/shard_map/ppermute | solution.py:26
  55.0 5.3 %collective-permute-start.2 = (f32[514,1]{1,0:T(8,128)S(1)}, f32[514,1]{1,0:T(8,128)S(1)}, u32[]{:S(2)}, u32[]{:S(2)}) collective-permute-start(f32[514,1]{1,0:T(8,128)S(1)} %get-tuple-element.16), channel_id=1, source_target_pairs={{0,1},{1,2},{2,3},{3,4},{4,5},{5,6},{6,7},{8,9},{9,10},{10,11},{11... | collective-permute-start | bytes 6176 | tf_op jit(solution)/shard_map/ppermute | solution.py:24
  56.9 7.7 %collective-permute-start.3 = (f32[514,1]{1,0:T(8,128)S(1)}, f32[514,1]{1,0:T(8,128)S(1)}, u32[]{:S(2)}, u32[]{:S(2)}) collective-permute-start(f32[514,1]{1,0:T(8,128)S(1)} %get-tuple-element.17), channel_id=1, source_target_pairs={{1,0},{2,1},{3,2},{4,3},{5,4},{6,5},{7,6},{9,8},{10,9},{11,10},{12... | collective-permute-start | bytes 6176 | tf_op jit(solution)/shard_map/ppermute | solution.py:26
  109.6 2.7 collective-permute-start.4
  111.1 4.3 %collective-permute-start.5 = (f32[1,512]{1,0:T(1,128)S(1)}, f32[1,512]{1,0:T(1,128)S(1)}, u32[]{:S(2)}, u32[]{:S(2)}) collective-permute-start(f32[1,512]{1,0:T(1,128)S(1)} %get-tuple-element.25), channel_id=1, source_target_pairs={{8,0},{16,8},{24,16},{9,1},{17,9},{25,17},{10,2},{18,10},{26,18},{... | collective-permute-start | bytes 6152 | tf_op jit(solution)/shard_map/ppermute | solution.py:26
  115.5 5.3 %collective-permute-start.6 = (f32[514,1]{1,0:T(8,128)S(1)}, f32[514,1]{1,0:T(8,128)S(1)}, u32[]{:S(2)}, u32[]{:S(2)}) collective-permute-start(f32[514,1]{1,0:T(8,128)S(1)} %get-tuple-element.14), channel_id=1, source_target_pairs={{0,1},{1,2},{2,3},{3,4},{4,5},{5,6},{6,7},{8,9},{9,10},{10,11},{11... | collective-permute-start | bytes 6176 | tf_op jit(solution)/shard_map/ppermute | solution.py:24
  117.5 7.7 %collective-permute-start.7 = (f32[514,1]{1,0:T(8,128)S(1)}, f32[514,1]{1,0:T(8,128)S(1)}, u32[]{:S(2)}, u32[]{:S(2)}) collective-permute-start(f32[514,1]{1,0:T(8,128)S(1)} %get-tuple-element.15), channel_id=1, source_target_pairs={{1,0},{2,1},{3,2},{4,3},{5,4},{6,5},{7,6},{9,8},{10,9},{11,10},{12... | collective-permute-start | bytes 6176 | tf_op jit(solution)/shard_map/ppermute | solution.py:26
  171.5 18.5 %copy-start.10 = (f32[512,512]{1,0:T(8,128)S(1)}, f32[512,512]{1,0:T(8,128)}, u32[]{:S(2)}) copy-start(f32[512,512]{1,0:T(8,128)} %param.6) | copy-start | bytes 3145732
  174.4 2.7 collective-permute-start.8
  175.8 4.3 %collective-permute-start.9 = (f32[1,512]{1,0:T(1,128)S(1)}, f32[1,512]{1,0:T(1,128)S(1)}, u32[]{:S(2)}, u32[]{:S(2)}) collective-permute-start(f32[1,512]{1,0:T(1,128)S(1)} %get-tuple-element.23), channel_id=1, source_target_pairs={{8,0},{16,8},{24,16},{9,1},{17,9},{25,17},{10,2},{18,10},{26,18},{... | collective-permute-start | bytes 6152 | tf_op jit(solution)/shard_map/ppermute | solution.py:26
  180.3 5.3 %collective-permute-start.10 = (f32[514,1]{1,0:T(8,128)S(1)}, f32[514,1]{1,0:T(8,128)S(1)}, u32[]{:S(2)}, u32[]{:S(2)}) collective-permute-start(f32[514,1]{1,0:T(8,128)S(1)} %get-tuple-element.12), channel_id=1, source_target_pairs={{0,1},{1,2},{2,3},{3,4},{4,5},{5,6},{6,7},{8,9},{9,10},{10,11},{11... | collective-permute-start | bytes 6176 | tf_op jit(solution)/shard_map/ppermute | solution.py:24
  182.2 7.7 %collective-permute-start.11 = (f32[514,1]{1,0:T(8,128)S(1)}, f32[514,1]{1,0:T(8,128)S(1)}, u32[]{:S(2)}, u32[]{:S(2)}) collective-permute-start(f32[514,1]{1,0:T(8,128)S(1)} %get-tuple-element.13), channel_id=1, source_target_pairs={{1,0},{2,1},{3,2},{4,3},{5,4},{6,5},{7,6},{9,8},{10,9},{11,10},{12... | collective-permute-start | bytes 6176 | tf_op jit(solution)/shard_map/ppermute | solution.py:26
  236.5 19.6 %copy-start.11 = (f32[512,512]{1,0:T(8,128)S(1)}, f32[512,512]{1,0:T(8,128)}, u32[]{:S(2)}) copy-start(f32[512,512]{1,0:T(8,128)} %param.6) | copy-start | bytes 3145732
  240.5 2.7 collective-permute-start.12
  241.9 4.3 %collective-permute-start.13 = (f32[1,512]{1,0:T(1,128)S(1)}, f32[1,512]{1,0:T(1,128)S(1)}, u32[]{:S(2)}, u32[]{:S(2)}) collective-permute-start(f32[1,512]{1,0:T(1,128)S(1)} %get-tuple-element.21), channel_id=1, source_target_pairs={{8,0},{16,8},{24,16},{9,1},{17,9},{25,17},{10,2},{18,10},{26,18},{... | collective-permute-start | bytes 6152 | tf_op jit(solution)/shard_map/ppermute | solution.py:26
  246.4 5.3 %collective-permute-start.14 = (f32[514,1]{1,0:T(8,128)S(1)}, f32[514,1]{1,0:T(8,128)S(1)}, u32[]{:S(2)}, u32[]{:S(2)}) collective-permute-start(f32[514,1]{1,0:T(8,128)S(1)} %get-tuple-element.10), channel_id=1, source_target_pairs={{0,1},{1,2},{2,3},{3,4},{4,5},{5,6},{6,7},{8,9},{9,10},{10,11},{11... | collective-permute-start | bytes 6176 | tf_op jit(solution)/shard_map/ppermute | solution.py:24
  248.3 7.7 %collective-permute-start.15 = (f32[514,1]{1,0:T(8,128)S(1)}, f32[514,1]{1,0:T(8,128)S(1)}, u32[]{:S(2)}, u32[]{:S(2)}) collective-permute-start(f32[514,1]{1,0:T(8,128)S(1)} %get-tuple-element.11), channel_id=1, source_target_pairs={{1,0},{2,1},{3,2},{4,3},{5,4},{6,5},{7,6},{9,8},{10,9},{11,10},{12... | collective-permute-start | bytes 6176 | tf_op jit(solution)/shard_map/ppermute | solution.py:26
  319.6 17.8 %copy-start.12 = (f32[512,512]{1,0:T(8,128)S(1)}, f32[512,512]{1,0:T(8,128)}, u32[]{:S(2)}) copy-start(f32[512,512]{1,0:T(8,128)} %param.6) | copy-start | bytes 3145732
  321.8 2.7 collective-permute-start.16
  323.3 4.3 %collective-permute-start.17 = (f32[1,512]{1,0:T(1,128)S(1)}, f32[1,512]{1,0:T(1,128)S(1)}, u32[]{:S(2)}, u32[]{:S(2)}) collective-permute-start(f32[1,512]{1,0:T(1,128)S(1)} %get-tuple-element.19), channel_id=1, source_target_pairs={{8,0},{16,8},{24,16},{9,1},{17,9},{25,17},{10,2},{18,10},{26,18},{... | collective-permute-start | bytes 6152 | tf_op jit(solution)/shard_map/ppermute | solution.py:26
  327.7 5.3 %collective-permute-start.18 = (f32[514,1]{1,0:T(8,128)S(1)}, f32[514,1]{1,0:T(8,128)S(1)}, u32[]{:S(2)}, u32[]{:S(2)}) collective-permute-start(f32[514,1]{1,0:T(8,128)S(1)} %get-tuple-element.8), channel_id=1, source_target_pairs={{0,1},{1,2},{2,3},{3,4},{4,5},{5,6},{6,7},{8,9},{9,10},{10,11},{11... | collective-permute-start | bytes 6176 | tf_op jit(solution)/shard_map/ppermute | solution.py:24
  329.7 7.7 %collective-permute-start.19 = (f32[514,1]{1,0:T(8,128)S(1)}, f32[514,1]{1,0:T(8,128)S(1)}, u32[]{:S(2)}, u32[]{:S(2)}) collective-permute-start(f32[514,1]{1,0:T(8,128)S(1)} %get-tuple-element.9), channel_id=1, source_target_pairs={{1,0},{2,1},{3,2},{4,3},{5,4},{6,5},{7,6},{9,8},{10,9},{11,10},{12... | collective-permute-start | bytes 6176 | tf_op jit(solution)/shard_map/ppermute | solution.py:26
  (15 other events, 167.5 us)
